TPU v7x, 32 devices: a whole 2x2x4 slice. The times are simulated.
32 devices in a mesh: dp: 8 (over y, x, core), dap: 4 (over z).
Axes of the slice: x: 2, y: 2, z: 4, core: 2. Of those that a mesh axis runs over, the one named last changes fastest.
Arguments:
- pair_act: bfloat16 [8, 128, 128, 128], P('dp', 'dap'), may hold values from -6 to 6
- pair_cot: bfloat16 [8, 128, 128, 128], P('dp', 'dap'), may hold values from -6 to 6
- in_gain: float32 [128], replicated, may hold values from 0.25 to 1.75
- in_bias: float32 [128], replicated, may hold values from -3 to 3
- proj_weight: bfloat16 [128, 512], replicated, may hold values from -0.5 to 0.5
- gate_weight: bfloat16 [128, 128], replicated, may hold values from -0.5 to 0.5
- out_gain: float32 [128], replicated, may hold values from 0.25 to 1.75
- out_bias: float32 [128], replicated, may hold values from -3 to 3
- out_weight: bfloat16 [128, 128], replicated, may hold values from -0.5 to 0.5
Outputs:
- update: bfloat16 [8, 128, 128, 128], P('dp', 'dap')
- pair_grad: bfloat16 [8, 128, 128, 128], P('dp', 'dap')
- proj_grad: float32 [128, 512], replicated
- gate_grad: float32 [128, 128], replicated
- out_grad: float32 [128, 128], replicated
- in_norm_grad: float32 [2, 128], replicated
- out_norm_grad: float32 [2, 128], replicated
All inputs are finite; a program needn't handle non-finite values.
Results may differ from a plain program's by a relative error of at most 0.0084.
Values may be sent and summed in bfloat16 or wider, within the bound.
A program may use at most 64 MiB of HBM per device.

v0:
```python
import jax
import jax.numpy as jnp
from jax import lax
from jax.sharding import PartitionSpec as P

epsilon = 1e-05


def norm_rows(values, along):
    row_mean = jnp.mean(values, axis=along, keepdims=True)
    centred = values - row_mean
    row_var = jnp.mean(centred * centred, axis=along, keepdims=True)
    inv_std = lax.rsqrt(row_var + epsilon)
    return (centred * inv_std, inv_std)


def norm_back(grad_hat, x_hat, inv_std, along):
    first = jnp.mean(grad_hat, axis=along, keepdims=True)
    second = jnp.mean(grad_hat * x_hat, axis=along, keepdims=True)
    return (grad_hat - first - x_hat * second) * inv_std


def backward_pieces(piece_d, piece_l, piece_r):
    back_l = jnp.einsum(
        "zhij,zhjk->zhik", piece_d, piece_r, preferred_element_type=jnp.float32
    ).astype(jnp.bfloat16)
    back_r = jnp.einsum(
        "zhij,zhik->zhjk", piece_d, piece_l, preferred_element_type=jnp.float32
    ).astype(jnp.bfloat16)
    return (back_l, back_r)


def shards(
    pair_act, pair_cot, in_gain, in_bias, proj_weight, gate_weight, out_gain, out_bias, out_weight
):
    f32 = jnp.float32
    bf16 = jnp.bfloat16
    groups = lax.axis_size("dap")
    row_count = pair_act.shape[1]
    crop_len = pair_act.shape[2]
    channels = pair_act.shape[3]
    hidden_w = out_weight.shape[0]
    per_dev = hidden_w // groups
    cell_count = row_count * crop_len
    scale = 1.0 / crop_len
    flat_act = pair_act.reshape(cell_count, channels).astype(f32)
    in_hat, in_inv = norm_rows(flat_act, 1)
    normed = (in_hat * in_gain + in_bias).astype(bf16)
    projected = jnp.einsum("mc,ch->hm", normed, proj_weight, preferred_element_type=f32)
    pre_ag = projected[0:hidden_w]
    pre_ap = projected[hidden_w : 2 * hidden_w]
    pre_bg = projected[2 * hidden_w : 3 * hidden_w]
    pre_bp = projected[3 * hidden_w : 4 * hidden_w]
    sig_a = jax.nn.sigmoid(pre_ag)
    sig_b = jax.nn.sigmoid(pre_bg)
    left_act = (sig_a * pre_ap).astype(bf16).reshape(groups, per_dev, row_count, crop_len)
    right_act = (sig_b * pre_bp).astype(bf16).reshape(groups, per_dev, row_count, crop_len)
    piece_l = lax.all_to_all(left_act, "dap", split_axis=0, concat_axis=2, tiled=True)
    piece_r = lax.all_to_all(right_act, "dap", split_axis=0, concat_axis=2, tiled=True)
    product = jnp.einsum("zhik,zhjk->zhij", piece_l, piece_r, preferred_element_type=f32).astype(
        bf16
    )
    returned = lax.all_to_all(product, "dap", split_axis=2, concat_axis=0, tiled=True)
    tri_out = returned.reshape(hidden_w, cell_count)
    tri_hat, tri_inv = norm_rows(tri_out.astype(f32), 0)
    tri_norm = (tri_hat * out_gain[:, None] + out_bias[:, None]).astype(bf16)
    gate_val = jax.nn.sigmoid(jnp.dot(normed, gate_weight, preferred_element_type=f32))
    mixed = jnp.einsum("hm,hc->mc", tri_norm, out_weight, preferred_element_type=f32)
    update = (gate_val * mixed).astype(bf16).reshape(1, row_count, crop_len, channels)
    cot_flat = pair_cot.reshape(cell_count, channels).astype(f32)
    d_mixed = (cot_flat * gate_val).astype(bf16)
    d_gate = (cot_flat * mixed * gate_val * (1.0 - gate_val)).astype(bf16)
    out_part = jnp.einsum("hm,mc->hc", tri_norm, d_mixed, preferred_element_type=f32) * scale
    gate_part = jnp.einsum("mc,md->cd", normed, d_gate, preferred_element_type=f32) * scale
    d_norm_out = jnp.einsum("mc,hc->hm", d_mixed, out_weight, preferred_element_type=f32)
    out_norm_part = (
        jnp.stack([jnp.sum(d_norm_out * tri_hat, axis=1), jnp.sum(d_norm_out, axis=1)]) * scale
    )
    d_tri = norm_back(d_norm_out * out_gain[:, None], tri_hat, tri_inv, 0).astype(bf16)
    d_tri = d_tri.reshape(groups, per_dev, row_count, crop_len)
    d_cols = lax.all_to_all(d_tri, "dap", split_axis=0, concat_axis=2, tiled=True)
    back_l, back_r = backward_pieces(d_cols, piece_l, piece_r)
    d_left, d_right = (
        lax.all_to_all(back_l, "dap", split_axis=2, concat_axis=0, tiled=True),
        lax.all_to_all(back_r, "dap", split_axis=2, concat_axis=0, tiled=True),
    )
    left_grad = d_left.reshape(hidden_w, cell_count).astype(f32)
    right_grad = d_right.reshape(hidden_w, cell_count).astype(f32)
    d_proj = jnp.concatenate(
        [
            left_grad * pre_ap * sig_a * (1.0 - sig_a),
            left_grad * sig_a,
            right_grad * pre_bp * sig_b * (1.0 - sig_b),
            right_grad * sig_b,
        ],
        axis=0,
    ).astype(bf16)
    proj_part = jnp.einsum("mc,hm->ch", normed, d_proj, preferred_element_type=f32) * scale
    d_normed = jnp.einsum(
        "hm,ch->mc", d_proj, proj_weight, preferred_element_type=f32
    ) + jnp.einsum("md,cd->mc", d_gate, gate_weight, preferred_element_type=f32)
    in_norm_part = (
        jnp.stack([jnp.sum(d_normed * in_hat, axis=0), jnp.sum(d_normed, axis=0)]) * scale
    )
    pair_grad = (
        norm_back(d_normed * in_gain, in_hat, in_inv, 1)
        .astype(bf16)
        .reshape(1, row_count, crop_len, channels)
    )
    proj_sum, gate_sum, out_sum, in_sum, outn_sum = lax.psum(
        (proj_part, gate_part, out_part, in_norm_part, out_norm_part), ("dp", "dap")
    )
    return (update, pair_grad, proj_sum, gate_sum, out_sum, in_sum, outn_sum)


def solution(mesh):
    placed = (
        P("dp", "dap", None, None),
        P("dp", "dap", None, None),
        P(),
        P(),
        P(),
        P(),
        P(),
        P(),
        P(),
    )
    return jax.shard_map(
        shards,
        mesh=mesh,
        in_specs=placed,
        out_specs=(P("dp", "dap", None, None), P("dp", "dap", None, None), P(), P(), P(), P(), P()),
        check_vma=False,
    )
```

profile of v0, /device:TPU:0, one launch (start us, length us, event | category | flops | bytes accessed | tf_op | source)
XLA Modules:
  0.0 383.8 jit_solution(13851624344998094155)
XLA Ops:
  7.2 1.7 convert_reduce_fusion
  8.9 2.3 multiply_reduce_fusion.3
  15.9 2.1 copy-done.1
  19.3 6.3 %all-to-all-start.1 = ((bf16[4,32,32,128]{3,2,1,0:T(8,128)(2,1)}), bf16[4,32,32,128]{3,2,1,0:T(8,128)(2,1)S(1)}, u32[]{:S(2)}, u32[]{:S(2)}) async-start(bf16[4,32,32,128]{3,2,1,0:T(8,128)(2,1)} %bitcast.157), calls=%async_computation.1 | async-start | bytes 2097152 | tf_op jit(solution)/shard_map/all_to_all | solution.py:59
  26.8 24.5 %all-to-all-done.1 = bf16[4,32,32,128]{3,2,1,0:T(8,128)(2,1)S(1)} async-done(((bf16[4,32,32,128]{3,2,1,0:T(8,128)(2,1)}), bf16[4,32,32,128]{3,2,1,0:T(8,128)(2,1)S(1)}, u32[]{:S(2)}, u32[]{:S(2)}) %all-to-all-start.1) | async-done | bytes 1048608 | tf_op jit(solution)/shard_map/all_to_all | solution.py:59
  51.4 4.3 %all-to-all-start = ((bf16[4,32,32,128]{3,2,1,0:T(8,128)(2,1)}), bf16[4,32,32,128]{3,2,1,0:T(8,128)(2,1)}, u32[]{:S(2)}, u32[]{:S(2)}) async-start(bf16[4,32,32,128]{3,2,1,0:T(8,128)(2,1)} %bitcast.156), calls=%async_computation | async-start | bytes 2097152 | tf_op jit(solution)/shard_map/all_to_all | solution.py:58
  55.8 25.2 %all-to-all-done = bf16[4,32,32,128]{3,2,1,0:T(8,128)(2,1)} async-done(((bf16[4,32,32,128]{3,2,1,0:T(8,128)(2,1)}), bf16[4,32,32,128]{3,2,1,0:T(8,128)(2,1)}, u32[]{:S(2)}, u32[]{:S(2)}) %all-to-all-start) | async-done | bytes 1048608 | tf_op jit(solution)/shard_map/all_to_all | solution.py:58
  83.9 27.7 %all_to_all.72 = bf16[1,32,128,128]{3,1,0,2:T(8,128)(2,1)S(1)} all-to-all(bf16[1,32,128,128]{3,1,0,2:T(8,128)(2,1)S(1)} %copy.34), channel_id=1, replica_groups=mesh['dp'=8,'dap'=4] {'dap'}, dimensions={2} | all-to-all | bytes 2097152 | tf_op jit(solution)/shard_map/all_to_all | solution.py:63
  114.5 3.0 copy.58
  117.5 1.9 copy.36
  119.4 2.3 add_convert_fusion
  124.3 2.7 fusion.6
  127.0 2.4 fusion.21
  130.8 4.1 %multiply_convert_fusion.1 = bf16[128,4096]{0,1:T(8,128)(2,1)} fusion(f32[4096,128]{1,0:T(8,128)S(1)} %get-tuple-element.34, f32[128,4096]{0,1:T(8,128)S(1)} %copy.36, f32[4096]{0:T(1024)S(1)} %get-tuple-element.36, f32[4096]{0:T(1024)S(1)} %get-tuple-element.37, f32[128]{0:T(128)S(1)} %copy-done.22, f32[4096]{0:T(1024)S(1)} %rsqrt_bitcast_fusion, ...), kind=kLoop, calls=%fused_computation.46 | loop fusion | flops 4194304 | bytes 5308928 | tf_op jit(solution)/shard_map/convert_element_type | solution.py:79
  136.6 27.8 %all_to_all.73 = bf16[4,32,32,128]{3,2,1,0:T(8,128)(2,1)S(1)} all-to-all(bf16[4,32,32,128]{3,2,1,0:T(8,128)(2,1)S(1)} %bitcast.159), channel_id=1, replica_groups=mesh['dp'=8,'dap'=4] {'dap'}, dimensions={0} | all-to-all | bytes 2097152 | tf_op jit(solution)/shard_map/all_to_all | solution.py:81
  165.0 1.7 copy.39
  166.6 4.3 %all-to-all-start.4 = ((bf16[1,32,128,128]{3,1,0,2:T(8,128)(2,1)}), bf16[1,32,128,128]{3,1,0,2:T(8,128)(2,1)}, u32[]{:S(2)}, u32[]{:S(2)}) async-start(bf16[1,32,128,128]{3,1,0,2:T(8,128)(2,1)} %copy.39), calls=%async_computation.4 | async-start | bytes 2097152 | tf_op jit(solution)/shard_map/all_to_all | solution.py:84
  171.4 1.7 copy.42
  173.1 22.6 %all-to-all-done.4 = bf16[1,32,128,128]{3,1,0,2:T(8,128)(2,1)} async-done(((bf16[1,32,128,128]{3,1,0,2:T(8,128)(2,1)}), bf16[1,32,128,128]{3,1,0,2:T(8,128)(2,1)}, u32[]{:S(2)}, u32[]{:S(2)}) %all-to-all-start.4) | async-done | bytes 1048608 | tf_op jit(solution)/shard_map/all_to_all | solution.py:84
  195.7 4.5 %all-to-all-start.5 = ((bf16[1,32,128,128]{3,1,0,2:T(8,128)(2,1)}), bf16[1,32,128,128]{3,1,0,2:T(8,128)(2,1)}, u32[]{:S(2)}, u32[]{:S(2)}) async-start(bf16[1,32,128,128]{3,1,0,2:T(8,128)(2,1)} %copy.42), calls=%async_computation.5 | async-start | bytes 2097152 | tf_op jit(solution)/shard_map/all_to_all | solution.py:85
  200.8 2.8 convolution_multiply_fusion.1
  204.7 2.9 copy.40
  207.7 17.9 %all-to-all-done.5 = bf16[1,32,128,128]{3,1,0,2:T(8,128)(2,1)} async-done(((bf16[1,32,128,128]{3,1,0,2:T(8,128)(2,1)}), bf16[1,32,128,128]{3,1,0,2:T(8,128)(2,1)}, u32[]{:S(2)}, u32[]{:S(2)}) %all-to-all-start.5) | async-done | bytes 1048608 | tf_op jit(solution)/shard_map/all_to_all | solution.py:85
  225.5 1.7 copy.43
  227.4 6.3 %fusion.13 = (bf16[128,4096]{1,0:T(8,128)(2,1)S(1)}, bf16[128,4096]{1,0:T(8,128)(2,1)S(1)}, bf16[128,4096]{1,0:T(8,128)(2,1)S(1)}, bf16[128,4096]{1,0:T(8,128)(2,1)S(1)}) fusion(f32[16,8,32,128]{3,2,1,0:T(8,128)S(1)} %bitcast.153, f32[512,4096]{1,0:T(8,128)} %copy-done.1, f32[16,8,32,128]{3,2,1,0:T(8,128)S(1)} %bitcast.154), kind=kLoop, calls=%fused_computation.23 | loop fusion | flops 10485760 | bytes 16777216 | tf_op jit(solution)/shard_map/convert.13
  235.4 2.2 convolution_multiply_fusion
  237.6 3.0 fusion.31
  240.6 2.4 multiply_reduce_fusion
  243.1 3.3 multiply_convert_fusion
  246.3 37.9 %all-reduce = (f32[2,128]{1,0:T(2,128)}, f32[2,128]{1,0:T(2,128)}) all-reduce(f32[2,128]{1,0:T(2,128)S(1)} %maximum_multiply_fusion, f32[2,128]{1,0:T(2,128)S(1)} %maximum_multiply_fusion.1), channel_id=1, replica_groups=mesh['dp'=8,'dap'=4] {'dp','dap'}, use_global_device_ids=true, to_apply=%region_13.0 | all-reduce | flops 512 | bytes 4096 | tf_op jit(solution)/shard_map/psum | solution.py:110
  284.3 88.0 %all-reduce.4.cloned.1.call-done = (f32[128,512]{1,0:T(8,128)}, f32[128,128]{1,0:T(8,128)}, f32[128,128]{1,0:T(8,128)}) async-done(((f32[128,512]{1,0:T(8,128)}, f32[128,128]{1,0:T(8,128)}, f32[128,128]{1,0:T(8,128)}), (f32[128,512]{1,0:T(8,128)}, f32[128,128]{1,0:T(8,128)}, f32[128,128]{1,0:T(8,128)})) %all-reduce.4.cloned.1.call-update) | async-done | bytes 393232 | tf_op jit(solution)/shard_map/psum | solution.py:110
  372.3 1.7 copy.62
  (87 shorter events, 26.1 us)
Async XLA Ops:
  7.2 6.4 %copy-start = (bf16[128,512]{1,0:T(8,128)(2,1)S(1)}, bf16[128,512]{1,0:T(8,128)(2,1)}, u32[]{:S(2)}) copy-start(bf16[128,512]{1,0:T(8,128)(2,1)} %param.13) | copy-start | bytes 393220
  7.2 4.1 %copy-start.2 = (bf16[1,32,128,128]{3,2,1,0:T(8,128)(2,1)S(1)}, bf16[1,32,128,128]{3,2,1,0:T(8,128)(2,1)}, u32[]{:S(2)}) copy-start(bf16[1,32,128,128]{3,2,1,0:T(8,128)(2,1)} %param.9) | copy-start | bytes 3145732
  7.2 4.1 %copy-start.23 = (f32[128]{0:T(128)S(1)}, f32[128]{0:T(128)}, u32[]{:S(2)}) copy-start(f32[128]{0:T(128)} %param.11) | copy-start | bytes 1540
  7.2 4.1 %copy-start.25 = (f32[128]{0:T(128)S(1)}, f32[128]{0:T(128)}, u32[]{:S(2)}) copy-start(f32[128]{0:T(128)} %param.12) | copy-start | bytes 1540
  12.6 1.0 copy-start.5
  14.8 3.2 copy-start.1
  19.3 32.1 %all-to-all-start.1 = ((bf16[4,32,32,128]{3,2,1,0:T(8,128)(2,1)}), bf16[4,32,32,128]{3,2,1,0:T(8,128)(2,1)S(1)}, u32[]{:S(2)}, u32[]{:S(2)}) async-start(bf16[4,32,32,128]{3,2,1,0:T(8,128)(2,1)} %bitcast.157), calls=%async_computation.1 | async-start | bytes 2097152 | tf_op jit(solution)/shard_map/all_to_all | solution.py:59
  51.4 29.6 %all-to-all-start = ((bf16[4,32,32,128]{3,2,1,0:T(8,128)(2,1)}), bf16[4,32,32,128]{3,2,1,0:T(8,128)(2,1)}, u32[]{:S(2)}, u32[]{:S(2)}) async-start(bf16[4,32,32,128]{3,2,1,0:T(8,128)(2,1)} %bitcast.156), calls=%async_computation | async-start | bytes 2097152 | tf_op jit(solution)/shard_map/all_to_all | solution.py:58
  55.8 27.4 %copy-start.10 = (bf16[1,32,4,32,128]{4,3,2,1,0:T(8,128)(2,1)}, bf16[1,32,4,32,128]{4,3,2,1,0:T(8,128)(2,1)S(1)}, u32[]{:S(2)}) copy-start(bf16[1,32,4,32,128]{4,3,2,1,0:T(8,128)(2,1)S(1)} %copy.33) | copy-start | bytes 3145732
  82.3 1.6 copy-start.8
  117.5 2.0 copy-start.22
  117.5 2.0 copy-start.24
  119.4 3.3 copy-start.20
  121.7 1.0 copy-start.12
  122.7 1.2 copy-start.6
  122.7 1.2 copy-start.21
  122.8 1.6 copy-start.26
  127.0 2.4 copy-start.16
  129.4 1.4 copy-start.3
  136.6 27.9 %copy-start.11 = (bf16[1,32,4,32,128]{4,3,2,1,0:T(8,128)(2,1)S(1)}, bf16[1,32,4,32,128]{4,3,2,1,0:T(8,128)(2,1)}, u32[]{:S(2)}) copy-start(bf16[1,32,4,32,128]{4,3,2,1,0:T(8,128)(2,1)} %copy-done.10) | copy-start | bytes 3145732
  165.0 5.9 %copy-start.9 = (bf16[1,32,4,32,128]{4,3,2,1,0:T(8,128)(2,1)S(1)}, bf16[1,32,4,32,128]{4,3,2,1,0:T(8,128)(2,1)}, u32[]{:S(2)}) copy-start(bf16[1,32,4,32,128]{4,3,2,1,0:T(8,128)(2,1)} %copy-done.8) | copy-start | bytes 3145732
  166.6 29.1 %all-to-all-start.4 = ((bf16[1,32,128,128]{3,1,0,2:T(8,128)(2,1)}), bf16[1,32,128,128]{3,1,0,2:T(8,128)(2,1)}, u32[]{:S(2)}, u32[]{:S(2)}) async-start(bf16[1,32,128,128]{3,1,0,2:T(8,128)(2,1)} %copy.39), calls=%async_computation.4 | async-start | bytes 2097152 | tf_op jit(solution)/shard_map/all_to_all | solution.py:84
  171.4 28.8 %copy-start.4 = (f32[4096,128]{1,0:T(8,128)S(1)}, f32[4096,128]{1,0:T(8,128)}, u32[]{:S(2)}) copy-start(f32[4096,128]{1,0:T(8,128)} %copy-done.3) | copy-start | bytes 6291460
  195.7 29.8 %all-to-all-start.5 = ((bf16[1,32,128,128]{3,1,0,2:T(8,128)(2,1)}), bf16[1,32,128,128]{3,1,0,2:T(8,128)(2,1)}, u32[]{:S(2)}, u32[]{:S(2)}) async-start(bf16[1,32,128,128]{3,1,0,2:T(8,128)(2,1)} %copy.42), calls=%async_computation.5 | async-start | bytes 2097152 | tf_op jit(solution)/shard_map/all_to_all | solution.py:85
  200.2 172.1 %all-reduce.4.cloned.1.call-start = ((), (), s32[]{:S(2)}) async-start(), calls=%async_computation.6 | async-start | bytes 786432 | tf_op jit(solution)/shard_map/psum | solution.py:110
  200.8 2.8 copy-start.7
  200.8 2.8 copy-start.14
  225.5 1.9 copy-start.13
  233.7 1.0 copy-start.17
  233.8 1.3 copy-start.18
  233.8 1.6 copy-start.19
  237.6 3.0 copy-start.15
Sparse Core Ops, SparseCore 0:
  243.2 129.0 all-reduce.3
where the time goes:
time: 385 us; the launch traced here: 384 us
  waiting for transfers between devices  178 us (46%)
  blocking collectives  93.5 us (24%)
  local copies, waits for them, and re-layouts  32.7 us (8%)
  other arithmetic  25.3 us (7%)
  matrix products  20.1 us (5%)
  starting transfers between devices  19.4 us (5%)
  between operations  14.6 us (4%)
    psum x1, waiting for transfers between devices, shards(): lax.psum((proj_part, gate_part, out_part, in_norm_part, out_norm_part), (...  88 us
    psum x1, blocking collectives, shards(): lax.psum((proj_part, gate_part, out_part, in_norm_part, out_norm_part), (...  37.9 us
    all_to_all x1, blocking collectives, shards(): lax.all_to_all(d_tri, 'dap', split_axis=0, concat_axis=2, tiled=True)  27.8 us
    all_to_all x1, blocking collectives, shards(): lax.all_to_all(product, 'dap', split_axis=2, concat_axis=0, tiled=True)  27.7 us
    all_to_all x1, waiting for transfers between devices, shards(): lax.all_to_all(left_act, 'dap', split_axis=0, concat_axis=2, tiled=True)  25.2 us
    all_to_all x1, waiting for transfers between devices, shards(): lax.all_to_all(right_act, 'dap', split_axis=0, concat_axis=2, tiled=True)  24.5 us
    all_to_all x1, waiting for transfers between devices, shards(): lax.all_to_all(back_l, 'dap', split_axis=2, concat_axis=0, tiled=True)  22.6 us
    unnamed x61, local copies, waits for them, and re-layouts  18.7 us
  transfers between devices with their start and end apart: 5, of which 5 were waited for; matrix products, arithmetic and copies ran while one was open for 4% of the time, Pallas kernels for 0%

commit v1 on v0

--- a/solution.py
+++ b/solution.py
@@ -108,7 +108,7 @@
         .reshape(1, row_count, crop_len, channels)
     )
     proj_sum, gate_sum, out_sum, in_sum, outn_sum = lax.psum(
-        (proj_part, gate_part, out_part, in_norm_part, out_norm_part), ("dp", "dap")
+        lax.psum((proj_part, gate_part, out_part, in_norm_part, out_norm_part), "dap"), "dp"
     )
     return (update, pair_grad, proj_sum, gate_sum, out_sum, in_sum, outn_sum)
 

time: 385 us -> 350 us (0.909)
  waiting for transfers between devices: 178 us -> 158 us
  blocking collectives: 93.5 us -> 78.1 us
    psum x1 -> x2, waiting for transfers between devices: 88 us -> 68.2 us  [the longest x1 36.4 us: shards(): lax.psum((proj_part, gate_part, out_part, in_norm_part, out_norm_part), '...]
    psum x1 -> x2, blocking collectives: 37.9 us -> 22.6 us  [the longest x1 12.3 us: shards(): lax.psum(lax.psum((proj_part, gate_part, out_part, in_norm_part, out_norm...]
  transfers between devices with their start and end apart: 5 -> 6, of which waited for: 5 -> 6; matrix products, arithmetic and copies ran while one was open for 4% -> 4% of each run, Pallas kernels for 0% -> 0%
where the time goes in v1:
time: 350 us; the launch traced here: 349 us
  waiting for transfers between devices  158 us (45%)
  blocking collectives  78.1 us (22%)
  local copies, waits for them, and re-layouts  32.7 us (9%)
  other arithmetic  25.3 us (7%)
  matrix products  20.1 us (6%)
  starting transfers between devices  19.4 us (6%)
  between operations  14.6 us (4%)
    psum x1, waiting for transfers between devices, shards(): lax.psum((proj_part, gate_part, out_part, in_norm_part, out_norm_part), '...  36.4 us
    psum x1, waiting for transfers between devices, shards(): lax.psum(lax.psum((proj_part, gate_part, out_part, in_norm_part, out_norm...  31.8 us
    all_to_all x1, blocking collectives, shards(): lax.all_to_all(d_tri, 'dap', split_axis=0, concat_axis=2, tiled=True)  27.8 us
    all_to_all x1, blocking collectives, shards(): lax.all_to_all(product, 'dap', split_axis=2, concat_axis=0, tiled=True)  27.7 us
    all_to_all x1, waiting for transfers between devices, shards(): lax.all_to_all(left_act, 'dap', split_axis=0, concat_axis=2, tiled=True)  25.2 us
    all_to_all x1, waiting for transfers between devices, shards(): lax.all_to_all(right_act, 'dap', split_axis=0, concat_axis=2, tiled=True)  24.5 us
    all_to_all x1, waiting for transfers between devices, shards(): lax.all_to_all(back_l, 'dap', split_axis=2, concat_axis=0, tiled=True)  22.6 us
    unnamed x61, local copies, waits for them, and re-layouts  18.7 us
  transfers between devices with their start and end apart: 6, of which 6 were waited for; matrix products, arithmetic and copies ran while one was open for 4% of the time, Pallas kernels for 0%

profile of v1, /device:TPU:0, one launch (start us, length us, event | category | flops | bytes accessed | tf_op | source)
XLA Modules:
  0.0 348.7 jit_solution(7741343542895835444)
XLA Ops:
  8.9 2.3 multiply_reduce_fusion.3
  15.9 2.1 copy-done.1
  19.3 6.3 %all-to-all-start.1 = ((bf16[4,32,32,128]{3,2,1,0:T(8,128)(2,1)}), bf16[4,32,32,128]{3,2,1,0:T(8,128)(2,1)S(1)}, u32[]{:S(2)}, u32[]{:S(2)}) async-start(bf16[4,32,32,128]{3,2,1,0:T(8,128)(2,1)} %bitcast.157), calls=%async_computation.1 | async-start | bytes 2097152 | tf_op jit(solution)/shard_map/all_to_all | solution.py:59
  26.8 24.5 %all-to-all-done.1 = bf16[4,32,32,128]{3,2,1,0:T(8,128)(2,1)S(1)} async-done(((bf16[4,32,32,128]{3,2,1,0:T(8,128)(2,1)}), bf16[4,32,32,128]{3,2,1,0:T(8,128)(2,1)S(1)}, u32[]{:S(2)}, u32[]{:S(2)}) %all-to-all-start.1) | async-done | bytes 1048608 | tf_op jit(solution)/shard_map/all_to_all | solution.py:59
  51.4 4.3 %all-to-all-start = ((bf16[4,32,32,128]{3,2,1,0:T(8,128)(2,1)}), bf16[4,32,32,128]{3,2,1,0:T(8,128)(2,1)}, u32[]{:S(2)}, u32[]{:S(2)}) async-start(bf16[4,32,32,128]{3,2,1,0:T(8,128)(2,1)} %bitcast.156), calls=%async_computation | async-start | bytes 2097152 | tf_op jit(solution)/shard_map/all_to_all | solution.py:58
  55.8 25.2 %all-to-all-done = bf16[4,32,32,128]{3,2,1,0:T(8,128)(2,1)} async-done(((bf16[4,32,32,128]{3,2,1,0:T(8,128)(2,1)}), bf16[4,32,32,128]{3,2,1,0:T(8,128)(2,1)}, u32[]{:S(2)}, u32[]{:S(2)}) %all-to-all-start) | async-done | bytes 1048608 | tf_op jit(solution)/shard_map/all_to_all | solution.py:58
  83.9 27.7 %all_to_all.72 = bf16[1,32,128,128]{3,1,0,2:T(8,128)(2,1)S(1)} all-to-all(bf16[1,32,128,128]{3,1,0,2:T(8,128)(2,1)S(1)} %copy.34), channel_id=1, replica_groups=mesh['dp'=8,'dap'=4] {'dap'}, dimensions={2} | all-to-all | bytes 2097152 | tf_op jit(solution)/shard_map/all_to_all | solution.py:63
  114.5 3.0 copy.58
  117.5 1.9 copy.36
  119.4 2.3 add_convert_fusion
  124.3 2.7 fusion.6
  127.0 2.4 fusion.21
  130.8 4.1 %multiply_convert_fusion.1 = bf16[128,4096]{0,1:T(8,128)(2,1)} fusion(f32[4096,128]{1,0:T(8,128)S(1)} %get-tuple-element.39, f32[128,4096]{0,1:T(8,128)S(1)} %copy.36, f32[4096]{0:T(1024)S(1)} %get-tuple-element.41, f32[4096]{0:T(1024)S(1)} %get-tuple-element.42, f32[128]{0:T(128)S(1)} %copy-done.22, f32[4096]{0:T(1024)S(1)} %rsqrt_bitcast_fusion, ...), kind=kLoop, calls=%fused_computation.46 | loop fusion | flops 4194304 | bytes 5308928 | tf_op jit(solution)/shard_map/convert_element_type | solution.py:79
  136.6 27.8 %all_to_all.73 = bf16[4,32,32,128]{3,2,1,0:T(8,128)(2,1)S(1)} all-to-all(bf16[4,32,32,128]{3,2,1,0:T(8,128)(2,1)S(1)} %bitcast.159), channel_id=1, replica_groups=mesh['dp'=8,'dap'=4] {'dap'}, dimensions={0} | all-to-all | bytes 2097152 | tf_op jit(solution)/shard_map/all_to_all | solution.py:81
  166.6 4.3 %all-to-all-start.4 = ((bf16[1,32,128,128]{3,1,0,2:T(8,128)(2,1)}), bf16[1,32,128,128]{3,1,0,2:T(8,128)(2,1)}, u32[]{:S(2)}, u32[]{:S(2)}) async-start(bf16[1,32,128,128]{3,1,0,2:T(8,128)(2,1)} %copy.39), calls=%async_computation.4 | async-start | bytes 2097152 | tf_op jit(solution)/shard_map/all_to_all | solution.py:84
  171.4 1.7 copy.42
  173.1 22.6 %all-to-all-done.4 = bf16[1,32,128,128]{3,1,0,2:T(8,128)(2,1)} async-done(((bf16[1,32,128,128]{3,1,0,2:T(8,128)(2,1)}), bf16[1,32,128,128]{3,1,0,2:T(8,128)(2,1)}, u32[]{:S(2)}, u32[]{:S(2)}) %all-to-all-start.4) | async-done | bytes 1048608 | tf_op jit(solution)/shard_map/all_to_all | solution.py:84
  195.7 4.5 %all-to-all-start.5 = ((bf16[1,32,128,128]{3,1,0,2:T(8,128)(2,1)}), bf16[1,32,128,128]{3,1,0,2:T(8,128)(2,1)}, u32[]{:S(2)}, u32[]{:S(2)}) async-start(bf16[1,32,128,128]{3,1,0,2:T(8,128)(2,1)} %copy.42), calls=%async_computation.5 | async-start | bytes 2097152 | tf_op jit(solution)/shard_map/all_to_all | solution.py:85
  200.8 2.8 convolution_multiply_fusion.1
  204.7 2.9 copy.40
  207.7 17.9 %all-to-all-done.5 = bf16[1,32,128,128]{3,1,0,2:T(8,128)(2,1)} async-done(((bf16[1,32,128,128]{3,1,0,2:T(8,128)(2,1)}), bf16[1,32,128,128]{3,1,0,2:T(8,128)(2,1)}, u32[]{:S(2)}, u32[]{:S(2)}) %all-to-all-start.5) | async-done | bytes 1048608 | tf_op jit(solution)/shard_map/all_to_all | solution.py:85
  225.5 1.7 copy.43
  227.4 6.3 %fusion.13 = (bf16[128,4096]{1,0:T(8,128)(2,1)S(1)}, bf16[128,4096]{1,0:T(8,128)(2,1)S(1)}, bf16[128,4096]{1,0:T(8,128)(2,1)S(1)}, bf16[128,4096]{1,0:T(8,128)(2,1)S(1)}) fusion(f32[16,8,32,128]{3,2,1,0:T(8,128)S(1)} %bitcast.153, f32[512,4096]{1,0:T(8,128)} %copy-done.1, f32[16,8,32,128]{3,2,1,0:T(8,128)S(1)} %bitcast.154), kind=kLoop, calls=%fused_computation.23 | loop fusion | flops 10485760 | bytes 16777216 | tf_op jit(solution)/shard_map/convert.13
  235.4 2.2 convolution_multiply_fusion
  237.6 3.0 fusion.31
  240.6 2.4 multiply_reduce_fusion
  243.1 36.4 %all-reduce.9.cloned.1.call-done = (f32[128,512]{1,0:T(8,128)}, f32[128,128]{1,0:T(8,128)}, f32[128,128]{1,0:T(8,128)}) async-done(((f32[128,512]{1,0:T(8,128)}, f32[128,128]{1,0:T(8,128)}, f32[128,128]{1,0:T(8,128)}), (f32[128,512]{1,0:T(8,128)}, f32[128,128]{1,0:T(8,128)}, f32[128,128]{1,0:T(8,128)})) %all-reduce.9.cloned.1.call-update) | async-done | bytes 393232 | tf_op jit(solution)/shard_map/psum | solution.py:111
  279.5 3.3 multiply_convert_fusion
  282.8 10.3 %all-reduce.2 = (f32[2,128]{1,0:T(2,128)S(1)}, f32[2,128]{1,0:T(2,128)S(1)}) all-reduce(f32[2,128]{1,0:T(2,128)S(1)} %maximum_multiply_fusion, f32[2,128]{1,0:T(2,128)S(1)} %maximum_multiply_fusion.1), channel_id=1, replica_groups=mesh['dp'=8,'dap'=4] {'dap'}, use_global_device_ids=true, to_apply=%region_16.0 | all-reduce | flops 512 | bytes 4096 | tf_op jit(solution)/shard_map/psum | solution.py:111
  293.1 12.3 %all-reduce = (f32[2,128]{1,0:T(2,128)}, f32[2,128]{1,0:T(2,128)}) all-reduce(f32[2,128]{1,0:T(2,128)S(1)} %get-tuple-element.19, f32[2,128]{1,0:T(2,128)S(1)} %get-tuple-element.20), channel_id=1, replica_groups=mesh['dp'=8,'dap'=4] {'dp'}, use_global_device_ids=true, to_apply=%region_17.0 | all-reduce | flops 512 | bytes 4096 | tf_op jit(solution)/shard_map/psum | solution.py:110
  305.4 31.8 %all-reduce.7.cloned.1.call-done = (f32[128,512]{1,0:T(8,128)}, f32[128,128]{1,0:T(8,128)}, f32[128,128]{1,0:T(8,128)}) async-done(((f32[128,512]{1,0:T(8,128)}, f32[128,128]{1,0:T(8,128)}, f32[128,128]{1,0:T(8,128)}), (f32[128,512]{1,0:T(8,128)}, f32[128,128]{1,0:T(8,128)}, f32[128,128]{1,0:T(8,128)})) %all-reduce.7.cloned.1.call-update) | async-done | bytes 393232 | tf_op jit(solution)/shard_map/psum | solution.py:110
  337.3 1.7 copy.65
  (91 shorter events, 29.5 us)
Async XLA Ops:
  7.2 6.4 %copy-start = (bf16[128,512]{1,0:T(8,128)(2,1)S(1)}, bf16[128,512]{1,0:T(8,128)(2,1)}, u32[]{:S(2)}) copy-start(bf16[128,512]{1,0:T(8,128)(2,1)} %param.13) | copy-start | bytes 393220
  7.2 4.1 %copy-start.2 = (bf16[1,32,128,128]{3,2,1,0:T(8,128)(2,1)S(1)}, bf16[1,32,128,128]{3,2,1,0:T(8,128)(2,1)}, u32[]{:S(2)}) copy-start(bf16[1,32,128,128]{3,2,1,0:T(8,128)(2,1)} %param.9) | copy-start | bytes 3145732
  7.2 4.1 %copy-start.23 = (f32[128]{0:T(128)S(1)}, f32[128]{0:T(128)}, u32[]{:S(2)}) copy-start(f32[128]{0:T(128)} %param.11) | copy-start | bytes 1540
  7.2 4.1 %copy-start.25 = (f32[128]{0:T(128)S(1)}, f32[128]{0:T(128)}, u32[]{:S(2)}) copy-start(f32[128]{0:T(128)} %param.12) | copy-start | bytes 1540
  14.8 3.2 copy-start.1
  19.3 32.1 %all-to-all-start.1 = ((bf16[4,32,32,128]{3,2,1,0:T(8,128)(2,1)}), bf16[4,32,32,128]{3,2,1,0:T(8,128)(2,1)S(1)}, u32[]{:S(2)}, u32[]{:S(2)}) async-start(bf16[4,32,32,128]{3,2,1,0:T(8,128)(2,1)} %bitcast.157), calls=%async_computation.1 | async-start | bytes 2097152 | tf_op jit(solution)/shard_map/all_to_all | solution.py:59
  51.4 29.6 %all-to-all-start = ((bf16[4,32,32,128]{3,2,1,0:T(8,128)(2,1)}), bf16[4,32,32,128]{3,2,1,0:T(8,128)(2,1)}, u32[]{:S(2)}, u32[]{:S(2)}) async-start(bf16[4,32,32,128]{3,2,1,0:T(8,128)(2,1)} %bitcast.156), calls=%async_computation | async-start | bytes 2097152 | tf_op jit(solution)/shard_map/all_to_all | solution.py:58
  55.8 27.4 %copy-start.10 = (bf16[1,32,4,32,128]{4,3,2,1,0:T(8,128)(2,1)}, bf16[1,32,4,32,128]{4,3,2,1,0:T(8,128)(2,1)S(1)}, u32[]{:S(2)}) copy-start(bf16[1,32,4,32,128]{4,3,2,1,0:T(8,128)(2,1)S(1)} %copy.33) | copy-start | bytes 3145732
  82.3 1.6 copy-start.8
  117.5 2.0 copy-start.22
  117.5 2.0 copy-start.24
  119.4 3.3 copy-start.20
  121.7 1.0 copy-start.12
  122.7 1.2 copy-start.6
  122.7 1.2 copy-start.21
  122.8 1.6 copy-start.26
  127.0 2.4 copy-start.16
  129.4 1.4 copy-start.3
  136.6 27.9 %copy-start.11 = (bf16[1,32,4,32,128]{4,3,2,1,0:T(8,128)(2,1)S(1)}, bf16[1,32,4,32,128]{4,3,2,1,0:T(8,128)(2,1)}, u32[]{:S(2)}) copy-start(bf16[1,32,4,32,128]{4,3,2,1,0:T(8,128)(2,1)} %copy-done.10) | copy-start | bytes 3145732
  165.0 5.9 %copy-start.9 = (bf16[1,32,4,32,128]{4,3,2,1,0:T(8,128)(2,1)S(1)}, bf16[1,32,4,32,128]{4,3,2,1,0:T(8,128)(2,1)}, u32[]{:S(2)}) copy-start(bf16[1,32,4,32,128]{4,3,2,1,0:T(8,128)(2,1)} %copy-done.8) | copy-start | bytes 3145732
  166.6 29.1 %all-to-all-start.4 = ((bf16[1,32,128,128]{3,1,0,2:T(8,128)(2,1)}), bf16[1,32,128,128]{3,1,0,2:T(8,128)(2,1)}, u32[]{:S(2)}, u32[]{:S(2)}) async-start(bf16[1,32,128,128]{3,1,0,2:T(8,128)(2,1)} %copy.39), calls=%async_computation.4 | async-start | bytes 2097152 | tf_op jit(solution)/shard_map/all_to_all | solution.py:84
  171.4 28.8 %copy-start.4 = (f32[4096,128]{1,0:T(8,128)S(1)}, f32[4096,128]{1,0:T(8,128)}, u32[]{:S(2)}) copy-start(f32[4096,128]{1,0:T(8,128)} %copy-done.3) | copy-start | bytes 6291460
  195.7 29.8 %all-to-all-start.5 = ((bf16[1,32,128,128]{3,1,0,2:T(8,128)(2,1)}), bf16[1,32,128,128]{3,1,0,2:T(8,128)(2,1)}, u32[]{:S(2)}, u32[]{:S(2)}) async-start(bf16[1,32,128,128]{3,1,0,2:T(8,128)(2,1)} %copy.42), calls=%async_computation.5 | async-start | bytes 2097152 | tf_op jit(solution)/shard_map/all_to_all | solution.py:85
  200.2 79.3 %all-reduce.9.cloned.1.call-start = ((), (), s32[]{:S(2)}) async-start(), calls=%async_computation.7 | async-start | bytes 786432 | tf_op jit(solution)/shard_map/psum | solution.py:111
  200.8 2.8 copy-start.7
  200.8 2.8 copy-start.14
  225.5 1.9 copy-start.13
  233.7 1.0 copy-start.17
  233.8 1.3 copy-start.18
  233.8 1.6 copy-start.19
  237.6 3.0 copy-start.15
  243.1 94.2 %all-reduce.7.cloned.1.call-start = ((), (), s32[]{:S(2)}) async-start(), calls=%async_computation.6 | async-start | bytes 786432 | tf_op jit(solution)/shard_map/psum | solution.py:110
  (1 other events, 1.0 us)
Sparse Core Ops, SparseCore 0:
  243.2 36.2 all-reduce.8
  282.9 54.3 all-reduce.6
